TPU v7x, 32 devices: a whole 2x2x4 slice. The times are simulated.
32 devices in a mesh: mem: 4 (over z), tile: 8 (over y, x, core).
Axes of the slice: x: 2, y: 2, z: 4, core: 2. Of those that a mesh axis runs over, the one named last changes fastest.
Arguments:
- state: float32 [20, 8, 12960], P('mem', 'tile'), may hold values from -6 to 6
- obs_index: int32 [8, 256], P('tile'), may hold values from 0 to 12959
- obs_count: int32 [8], P('tile'), may hold values from 32 to 256, as said below
- obs_value: float32 [8, 256], P('tile'), may hold values from -8 to 8
- obs_rinv: float32 [8, 256], P('tile'), may hold values from 0.1 to 1
- radius: int32 [8], P('tile'), may hold values from 1 to 2
Outputs:
- analysis: float32 [20, 8, 12960], P('mem', 'tile')
Inputs may be any that keep to these rules, and one draw needn't show every extreme that they name: `obs_count`: at most 256; some tile has exactly 256 in every draw.
All inputs are finite; a program needn't handle non-finite values.
Results may differ from a plain program's by a relative error of at most 0.0003.
Values sent between devices are 32-bit elements; how exact they have to be, the bound alone decides.
A program may use at most 64 MiB of HBM per device.

v0:
```python
import jax
import jax.numpy as jnp
from jax import lax
from jax.sharding import PartitionSpec as P

COLS = 45
BLOCK = 9
HALO = 2
NS_ITERS = 4
highest = lax.Precision.HIGHEST


def shifted(block, axis, distance):
    devices = range(lax.axis_size(axis))
    route = [((i - distance) % len(devices), i) for i in devices]
    return lax.ppermute(block, axis, route)


def block_points(band_id, tile_id, rows_dev):
    half_block = (BLOCK - 1) // 2
    row_blocks = rows_dev // BLOCK
    col_blocks = COLS // BLOCK
    row_ids = band_id * rows_dev + BLOCK * jnp.arange(row_blocks, dtype=jnp.int32) + half_block
    col_ids = tile_id * COLS + BLOCK * jnp.arange(col_blocks, dtype=jnp.int32) + half_block
    point_rows = (
        jnp.broadcast_to(row_ids[:, None], (row_blocks, col_blocks)).reshape(-1).astype(jnp.float32)
    )
    point_cols = (
        jnp.broadcast_to(col_ids[None, :], (row_blocks, col_blocks)).reshape(-1).astype(jnp.float32)
    )
    return (point_rows, point_cols)


def locality(obs_meta, point_rows, point_cols, extent, circle):
    row_gap = jnp.abs(obs_meta[2][None, :] - point_rows[:, None])
    col_gap = jnp.abs(obs_meta[3][None, :] - point_cols[:, None])
    col_gap = jnp.minimum(col_gap, circle - col_gap)
    taper = jnp.maximum(0.0, 1.0 - row_gap / extent) * jnp.maximum(0.0, 1.0 - col_gap / extent)
    return taper * obs_meta[1][None, :]


def add_block(totals, ens_blk, meta_blk, point_rows, point_cols, extent, circle):
    gram_sum, rhs_sum = totals
    centre = jnp.mean(ens_blk, axis=0)
    spread_obs = ens_blk - centre[None, :]
    innovation = meta_blk[0] - centre
    weights = locality(meta_blk, point_rows, point_cols, extent, circle)
    weighted = weights[:, None, :] * spread_obs[None, :, :]
    gram_sum = gram_sum + jnp.einsum("pkj,lj->pkl", weighted, spread_obs, precision=highest)
    rhs_sum = rhs_sum + jnp.einsum("pkj,j->pk", weighted, innovation, precision=highest)
    return (gram_sum, rhs_sum)


def transform(gram_sum, rhs_sum, members):
    identity = jnp.eye(members, dtype=jnp.float32)
    gram_full = gram_sum + (members - 1.0) * identity[None]
    frob_norm = jnp.sqrt(jnp.sum(gram_full * gram_full, axis=(1, 2)))
    iterate = gram_full / frob_norm[:, None, None]
    inv_root = jnp.broadcast_to(identity, gram_full.shape)
    for sweep in range(NS_ITERS):
        middle = 1.5 * identity[None] - 0.5 * jnp.einsum(
            "pij,pjk->pik", inv_root, iterate, precision=highest
        )
        iterate = jnp.einsum("pij,pjk->pik", iterate, middle, precision=highest)
        inv_root = jnp.einsum("pij,pjk->pik", middle, inv_root, precision=highest)
    inv_root = inv_root / jnp.sqrt(frob_norm)[:, None, None]
    inner = jnp.einsum("pij,pj->pi", inv_root, rhs_sum, precision=highest)
    mean_shift = jnp.einsum("pij,pj->pi", inv_root, inner, precision=highest)
    return jnp.sqrt(members - 1.0) * inv_root + mean_shift[:, :, None]


def apply_mix(band_state, mixing, rows_dev):
    members = band_state.shape[0]
    row_blocks = rows_dev // BLOCK
    col_blocks = COLS // BLOCK
    cell_grid = band_state.reshape(members, row_blocks, BLOCK, col_blocks, BLOCK)
    centre = jnp.mean(cell_grid, axis=0)
    spread_state = cell_grid - centre[None]
    mix_blocks = mixing.reshape(row_blocks, col_blocks, members, members)
    result = (
        jnp.einsum("ablk,laibj->kaibj", mix_blocks, spread_state, precision=highest) + centre[None]
    )
    return result.reshape(members, rows_dev * COLS)


def shards(state, obs_index, obs_count, obs_value, obs_rinv, radius):
    groups = lax.axis_size("mem")
    tile_count = lax.axis_size("tile")
    mem_dev = state.shape[0]
    cell_count = state.shape[2]
    members = mem_dev * groups
    band_cells = cell_count // groups
    rows_dev = band_cells // COLS
    circle = 1.0 * COLS * tile_count
    tile_id = lax.axis_index("tile")
    band_id = lax.axis_index("mem")
    slot_count = obs_index.shape[1]
    own_state = state[:, 0, :]
    cell_index = obs_index[0]
    own_obs = jnp.take(own_state, cell_index, axis=1)
    slot_ids = jnp.arange(slot_count, dtype=jnp.int32)
    rinv_live = jnp.where(slot_ids < obs_count[0], obs_rinv[0], 0.0)
    obs_row = (cell_index // COLS).astype(jnp.float32)
    obs_col = (cell_index % COLS + tile_id * COLS).astype(jnp.float32)
    obs_meta = jnp.stack([obs_value[0], rinv_live, obs_row, obs_col])
    offsets = [distance * direction for distance in range(1, HALO + 1) for direction in (1, -1)]
    ensemble = lax.all_gather(own_obs, "mem", axis=0, tiled=True)
    local_rows = jnp.concatenate([ensemble, obs_meta], axis=0)
    pieces = [local_rows]
    for offset in offsets:
        pieces.append(shifted(local_rows, "tile", offset))
    window = jnp.concatenate(pieces, axis=1)
    ens_win = window[:members]
    meta_win = window[members:]
    spread = state.reshape(mem_dev, groups, band_cells)
    gathered_state = lax.all_to_all(spread, "mem", split_axis=1, concat_axis=0, tiled=True)
    point_rows, point_cols = block_points(band_id, tile_id, rows_dev)
    extent = (radius[0] * COLS).astype(jnp.float32)
    points = point_rows.shape[0]
    stride = min(128, slot_count)
    per_piece = slot_count // stride
    segments = len(pieces)
    totals = (
        jnp.zeros((points, members, members), jnp.float32),
        jnp.zeros((points, members), jnp.float32),
    )

    def visit(block_id, carried):
        first_col = block_id * stride
        ens_blk = lax.dynamic_slice_in_dim(ens_win, first_col, stride, 1)
        meta_blk = lax.dynamic_slice_in_dim(meta_win, first_col, stride, 1)
        return add_block(carried, ens_blk, meta_blk, point_rows, point_cols, extent, circle)

    for segment in range(segments):
        weights_row = meta_win[1, segment * slot_count : (segment + 1) * slot_count]
        filled = jnp.sum((weights_row > 0.0).astype(jnp.int32))
        opening = segment * per_piece
        totals = lax.fori_loop(opening, opening + (filled + stride - 1) // stride, visit, totals)
    mixing = transform(totals[0], totals[1], members)
    analysis = apply_mix(gathered_state[:, 0, :], mixing, rows_dev)
    returned = lax.all_to_all(analysis[:, None, :], "mem", split_axis=0, concat_axis=1, tiled=True)
    return returned.reshape(mem_dev, 1, cell_count)


def solution(mesh):
    in_specs = (
        P("mem", "tile", None),
        P("tile", None),
        P("tile"),
        P("tile", None),
        P("tile", None),
        P("tile"),
    )
    out_specs = P("mem", "tile", None)
    return jax.shard_map(shards, mesh=mesh, in_specs=in_specs, out_specs=out_specs, check_vma=False)
```

profile of v0, /device:TPU:5, one launch (start us, length us, event | category | flops | bytes accessed | tf_op | source)
XLA Modules:
  0.0 104.6 jit_solution(1941645143184801129)
XLA Ops:
  0.7 5.1 %copy.32 = f32[5,1,12960]{0,2,1:T(8,128)} copy(f32[5,1,12960]{2,1,0:T(1,128)} %param.16) | data formatting | bytes 518400 | tf_op args[0]
  5.8 3.6 %gather_fusion = f32[256,5]{1,0:T(8,128)S(1)} fusion(f32[5,12960]{0,1:T(8,128)} %bitcast.212, s32[1024]{0:T(1024)S(1)} %pad_clamp_fusion), kind=kCustom, calls=%fused_computation | custom fusion | bytes 11264 | tf_op jit(solution)/shard_map/jit(_take)/gather | solution.py:100
  9.6 10.8 %all-gather = f32[4,5,256]{2,1,0:T(8,128)S(1)} all-gather(f32[1,5,256]{2,1,0:T(8,128)S(1)} %copy.33), channel_id=1, replica_groups=mesh['mem'=4,'tile'=8] {'mem'}, dimensions={0}, use_global_device_ids=true | all-gather | bytes 25600 | tf_op jit(solution)/shard_map/all_gather | solution.py:107
  21.1 1.2 %collective-permute-start.3 = (f32[24,256]{1,0:T(8,128)S(1)}, f32[24,256]{1,0:T(8,128)S(1)}, u32[]{:S(2)}, u32[]{:S(2)}) collective-permute-start(f32[24,256]{1,0:T(8,128)S(1)} %concatenate.6), channel_id=1, source_target_pairs={{2,0},{3,1},{4,2},{5,3},{6,4},{7,5},{0,6},{1,7},{10,8},{11,9},{12,... | collective-permute-start | bytes 73736 | tf_op jit(solution)/shard_map/ppermute | solution.py:16
  22.7 3.8 %collective-permute-start.1 = (f32[24,256]{1,0:T(8,128)S(1)}, f32[24,256]{1,0:T(8,128)S(1)}, u32[]{:S(2)}, u32[]{:S(2)}) collective-permute-start(f32[24,256]{1,0:T(8,128)S(1)} %concatenate.6), channel_id=1, source_target_pairs={{1,0},{2,1},{3,2},{4,3},{5,4},{6,5},{7,6},{0,7},{9,8},{10,9},{11,1... | collective-permute-start | bytes 73736 | tf_op jit(solution)/shard_map/ppermute | solution.py:16
  26.5 2.0 %collective-permute-start = (f32[24,256]{1,0:T(8,128)S(1)}, f32[24,256]{1,0:T(8,128)S(1)}, u32[]{:S(2)}, u32[]{:S(2)}) collective-permute-start(f32[24,256]{1,0:T(8,128)S(1)} %concatenate.6), channel_id=1, source_target_pairs={{7,0},{0,1},{1,2},{2,3},{3,4},{4,5},{5,6},{6,7},{15,8},{8,9},{9,10... | collective-permute-start | bytes 73736 | tf_op jit(solution)/shard_map/ppermute | solution.py:16
  30.2 4.3 %all-to-all-start = ((f32[5,4,3240]{2,0,1:T(8,128)}), f32[5,4,3240]{2,0,1:T(8,128)S(1)}, u32[]{:S(2)}, u32[]{:S(2)}) async-start(f32[5,4,3240]{2,0,1:T(8,128)} %copy.29), calls=%async_computation | async-start | bytes 851968 | tf_op jit(solution)/shard_map/all_to_all | solution.py:116
  41.6 2.6 %while.65 = (s32[]{:T(128)}, f32[40,20,20]{0,2,1:T(8,128)S(1)}, f32[40,20]{0,1:T(8,128)S(1)}, s32[]{:T(128)}, f32[4,1280]{1,0:T(4,128)S(1)}, /*index=5*/f32[]{:T...) while((s32[]{:T(128)}, f32[40,20,20]{0,2,1:T(8,128)S(1)}, ...), condition=%wide.region_4.5_spmd.clone, body=%wide.region_2.4_spmd.clone.sunk | while | flops 26103460 | bytes 275183 | solution.py:138
  42.7 1.5 %convolution_add_fusion.10 = f32[40,20,20]{0,2,1:T(8,128)S(1)} fusion(f32[40,20,20]{0,2,1:T(8,128)S(1)} %get-tuple-element.817, f32[20,128]{1,0:T(8,128)S(1)} %dynamic-slice_subtract_fusion.10, f32[40,128]{1,0:T(8,128)S(1)} %fusion.183), kind=kOutput, calls=%fused_computation.11.clone.1 | convolution fusion | flops 24694400 | bytes 158720 | tf_op jit(solution)/shard_map/while/body/pkj,lj->pkl/dot_general | solution.py:49
  44.2 2.6 %while.66 = (s32[]{:T(128)}, f32[40,20,20]{0,2,1:T(8,128)S(1)}, f32[40,20]{0,1:T(8,128)S(1)}, s32[]{:T(128)}, f32[4,1280]{1,0:T(4,128)S(1)}, /*index=5*/f32[]{:T...) while((s32[]{:T(128)}, f32[40,20,20]{0,2,1:T(8,128)S(1)}, ...), condition=%wide.region_8.9_spmd.clone, body=%wide.region_6.8_spmd.clone.sunk | while | flops 26103460 | bytes 275183 | solution.py:138
  45.3 1.5 %convolution_add_fusion.11 = f32[40,20,20]{0,2,1:T(8,128)S(1)} fusion(f32[40,20,20]{0,2,1:T(8,128)S(1)} %get-tuple-element.856, f32[20,128]{1,0:T(8,128)S(1)} %dynamic-slice_subtract_fusion.11, f32[40,128]{1,0:T(8,128)S(1)} %fusion.189), kind=kOutput, calls=%fused_computation.37.clone.1 | convolution fusion | flops 24694400 | bytes 158720 | tf_op jit(solution)/shard_map/while/body/pkj,lj->pkl/dot_general | solution.py:49
  46.9 2.6 %while.67 = (s32[]{:T(128)}, f32[40,20,20]{0,2,1:T(8,128)S(1)}, f32[40,20]{0,1:T(8,128)S(1)}, s32[]{:T(128)}, f32[4,1280]{1,0:T(4,128)S(1)}, /*index=5*/f32[]{:T...) while((s32[]{:T(128)}, f32[40,20,20]{0,2,1:T(8,128)S(1)}, ...), condition=%wide.region_12.13_spmd.clone, body=%wide.region_10.12_spmd.clone.sunk | while | flops 26103460 | bytes 275183 | solution.py:138
  48.0 1.5 %convolution_add_fusion.12 = f32[40,20,20]{0,2,1:T(8,128)S(1)} fusion(f32[40,20,20]{0,2,1:T(8,128)S(1)} %get-tuple-element.895, f32[20,128]{1,0:T(8,128)S(1)} %dynamic-slice_subtract_fusion.12, f32[40,128]{1,0:T(8,128)S(1)} %fusion.195), kind=kOutput, calls=%fused_computation.63.clone.1 | convolution fusion | flops 24694400 | bytes 158720 | tf_op jit(solution)/shard_map/while/body/pkj,lj->pkl/dot_general | solution.py:49
  49.5 5.3 %while.68 = (s32[]{:T(128)}, f32[40,20,20]{0,2,1:T(8,128)S(1)}, f32[40,20]{0,1:T(8,128)S(1)}, s32[]{:T(128)}, f32[4,1280]{1,0:T(4,128)S(1)}, /*index=5*/f32[]{:T...) while((s32[]{:T(128)}, f32[40,20,20]{0,2,1:T(8,128)S(1)}, ...), condition=%wide.region_16.17_spmd.clone, body=%wide.region_14.16_spmd.clone.sunk | while | flops 26103460 | bytes 275183 | solution.py:138
  50.6 1.5 %convolution_add_fusion.13 = f32[40,20,20]{0,2,1:T(8,128)S(1)} fusion(f32[40,20,20]{0,2,1:T(8,128)S(1)} %get-tuple-element.934, f32[20,128]{1,0:T(8,128)S(1)} %dynamic-slice_subtract_fusion.13, f32[40,128]{1,0:T(8,128)S(1)} %fusion.201), kind=kOutput, calls=%fused_computation.89.clone.1 | convolution fusion | flops 24694400 | bytes 158720 | tf_op jit(solution)/shard_map/while/body/pkj,lj->pkl/dot_general | solution.py:49
  53.3 1.5 %convolution_add_fusion.13 = f32[40,20,20]{0,2,1:T(8,128)S(1)} fusion(f32[40,20,20]{0,2,1:T(8,128)S(1)} %get-tuple-element.934, f32[20,128]{1,0:T(8,128)S(1)} %dynamic-slice_subtract_fusion.13, f32[40,128]{1,0:T(8,128)S(1)} %fusion.201), kind=kOutput, calls=%fused_computation.89.clone.1 | convolution fusion | flops 24694400 | bytes 158720 | tf_op jit(solution)/shard_map/while/body/pkj,lj->pkl/dot_general | solution.py:49
  54.8 2.8 %while.69 = (s32[]{:T(128)}, f32[40,20,20]{0,2,1:T(8,128)S(1)}, f32[40,20]{0,1:T(8,128)S(1)}, s32[]{:T(128)}, f32[4,1280]{1,0:T(4,128)S(1)}, /*index=5*/f32[]{:T...) while((s32[]{:T(128)}, f32[40,20,20]{0,2,1:T(8,128)S(1)}, ...), condition=%wide.region_20.21_spmd.clone, body=%wide.region_18.20_spmd.clone.sunk | while | flops 26103460 | bytes 275183 | solution.py:138
  55.9 1.5 %convolution_add_fusion.14 = f32[40,20,20]{0,2,1:T(8,128)S(1)} fusion(f32[40,20,20]{0,2,1:T(8,128)S(1)} %get-tuple-element.973, f32[20,128]{1,0:T(8,128)S(1)} %dynamic-slice_subtract_fusion.14, f32[40,128]{1,0:T(8,128)S(1)} %fusion.207), kind=kOutput, calls=%fused_computation.115.clone.1 | convolution fusion | flops 24694400 | bytes 158720 | tf_op jit(solution)/shard_map/while/body/pkj,lj->pkl/dot_general | solution.py:49
  72.0 3.7 %reshape_squeeze.3 = f32[20,8,9,5,9]{4,3,2,1,0:T(8,128)} reshape(f32[4,5,1,3240]{3,1,0,2:T(8,128)S(1)} %bitcast.213) | data formatting | bytes 518400 | tf_op jit(solution)/shard_map/reshape;squeeze | solution.py:76
  75.7 4.9 %copy.31 = f32[20,8,9,5,9]{0,4,2,3,1:T(8,128)S(1)} copy(f32[20,8,9,5,9]{4,3,2,1,0:T(8,128)} %reshape_squeeze.3) | data formatting | bytes 518400 | tf_op jit(solution)/shard_map/reshape;squeeze | solution.py:76
  82.0 4.5 %bitcast_add_fusion.5 = f32[20,8,9,5,9]{0,4,2,3,1:T(8,128)S(1)} fusion(f32[8,5,20,20,1]{3,2,4,1,0:T(8,128)} %bitcast.215, f32[20,8,9,5,9]{0,4,2,3,1:T(8,128)S(1)} %copy.31, f32[8,9,5,9]{3,1,2,0:T(8,128)S(1)} %copy.30), kind=kOutput, calls=%fused_computation.141 | convolution fusion | flops 15681600 | bytes 595360 | tf_op jit(solution)/shard_map/ablk,laibj->kaibj/dot_general | solution.py:81
  86.7 1.4 %broadcast_in_dim_reshape.3 = f32[20,1,3240]{0,2,1:T(8,128)} reshape(f32[20,8,9,5,9]{0,4,3,2,1:T(8,128)S(1)} %copy.36) | data formatting | bytes 518400 | tf_op jit(solution)/shard_map/broadcast_in_dim;reshape | solution.py:141
  88.1 1.8 %copy.37 = f32[20,1,3240]{2,1,0:T(1,128)S(1)} copy(f32[20,1,3240]{0,2,1:T(8,128)} %broadcast_in_dim_reshape.3) | data formatting | bytes 518400 | tf_op jit(solution)/shard_map/broadcast_in_dim;reshape | solution.py:141
  89.9 13.5 %all_to_all.30 = f32[20,1,3240]{2,1,0:T(1,128)S(1)} all-to-all(f32[20,1,3240]{2,1,0:T(1,128)S(1)} %copy.37), channel_id=1, replica_groups=mesh['mem'=4,'tile'=8] {'mem'}, dimensions={0} | all-to-all | bytes 518400 | tf_op jit(solution)/shard_map/all_to_all | solution.py:141
  (148 shorter events, 29.3 us)
Async XLA Ops:
  0.7 5.1 %copy-start.2 = (s32[1,256]{1,0:T(1,128)S(1)}, s32[1,256]{1,0:T(1,128)}, u32[]{:S(2)}) copy-start(s32[1,256]{1,0:T(1,128)} %param.17) | copy-start | bytes 3076
  0.7 19.7 %copy-start.3 = (f32[1,256]{1,0:T(1,128)S(1)}, f32[1,256]{1,0:T(1,128)}, u32[]{:S(2)}) copy-start(f32[1,256]{1,0:T(1,128)} %param.20) | copy-start | bytes 3076
  0.7 20.4 %copy-start.4 = (f32[1,256]{1,0:T(1,128)S(1)}, f32[1,256]{1,0:T(1,128)}, u32[]{:S(2)}) copy-start(f32[1,256]{1,0:T(1,128)} %param.19) | copy-start | bytes 3076
  0.7 27.8 %copy-start.1 = (f32[5,1,12960]{2,1,0:T(1,128)S(1)}, f32[5,1,12960]{2,1,0:T(1,128)}, u32[]{:S(2)}) copy-start(f32[5,1,12960]{2,1,0:T(1,128)} %param.16) | copy-start | bytes 777604
  21.1 14.8 %collective-permute-start.3 = (f32[24,256]{1,0:T(8,128)S(1)}, f32[24,256]{1,0:T(8,128)S(1)}, u32[]{:S(2)}, u32[]{:S(2)}) collective-permute-start(f32[24,256]{1,0:T(8,128)S(1)} %concatenate.6), channel_id=1, source_target_pairs={{2,0},{3,1},{4,2},{5,3},{6,4},{7,5},{0,6},{1,7},{10,8},{11,9},{12,... | collective-permute-start | bytes 73736 | tf_op jit(solution)/shard_map/ppermute | solution.py:16
  22.3 14.3 %collective-permute-start.2 = (f32[24,256]{1,0:T(8,128)S(1)}, f32[24,256]{1,0:T(8,128)S(1)}, u32[]{:S(2)}, u32[]{:S(2)}) collective-permute-start(f32[24,256]{1,0:T(8,128)S(1)} %concatenate.6), channel_id=1, source_target_pairs={{6,0},{7,1},{0,2},{1,3},{2,4},{3,5},{4,6},{5,7},{14,8},{15,9},{8,1... | collective-permute-start | bytes 73736 | tf_op jit(solution)/shard_map/ppermute | solution.py:16
  22.7 14.7 %collective-permute-start.1 = (f32[24,256]{1,0:T(8,128)S(1)}, f32[24,256]{1,0:T(8,128)S(1)}, u32[]{:S(2)}, u32[]{:S(2)}) collective-permute-start(f32[24,256]{1,0:T(8,128)S(1)} %concatenate.6), channel_id=1, source_target_pairs={{1,0},{2,1},{3,2},{4,3},{5,4},{6,5},{7,6},{0,7},{9,8},{10,9},{11,1... | collective-permute-start | bytes 73736 | tf_op jit(solution)/shard_map/ppermute | solution.py:16
  26.5 13.5 %collective-permute-start = (f32[24,256]{1,0:T(8,128)S(1)}, f32[24,256]{1,0:T(8,128)S(1)}, u32[]{:S(2)}, u32[]{:S(2)}) collective-permute-start(f32[24,256]{1,0:T(8,128)S(1)} %concatenate.6), channel_id=1, source_target_pairs={{7,0},{0,1},{1,2},{2,3},{3,4},{4,5},{5,6},{6,7},{15,8},{8,9},{9,10... | collective-permute-start | bytes 73736 | tf_op jit(solution)/shard_map/ppermute | solution.py:16
  30.2 41.1 %all-to-all-start = ((f32[5,4,3240]{2,0,1:T(8,128)}), f32[5,4,3240]{2,0,1:T(8,128)S(1)}, u32[]{:S(2)}, u32[]{:S(2)}) async-start(f32[5,4,3240]{2,0,1:T(8,128)} %copy.29), calls=%async_computation | async-start | bytes 851968 | tf_op jit(solution)/shard_map/all_to_all | solution.py:116
  71.3 0.8 copy-start
where the time goes:
time: 105 us
  matrix products  28.1 us (27%)
  local copies, waits for them, and re-layouts  27.2 us (26%)
  blocking collectives  24.2 us (23%)
  starting transfers between devices  11.7 us (11%)
  other arithmetic  7.44 us (7%)
  between operations  5.13 us (5%)
    all_to_all x1, blocking collectives, shards(): lax.all_to_all(analysis[:, None, :], 'mem', split_axis=0, concat_axis=1,...  13.5 us
    all_gather x1, blocking collectives, shards(): ensemble = lax.all_gather(own_obs, 'mem', axis=0, tiled=True)  10.8 us
    dot_general x6, matrix products, add_block(): jnp.einsum('pkj,lj->pkl', weighted, spread_obs, precision=highest)  8.91 us
    another operation x2, local copies, waits for them, and re-layouts, apply_mix(): band_state.reshape(members, row_blocks, BLOCK, col_blocks, BLOCK)  8.62 us
    ppermute x4, starting transfers between devices, shifted(): return lax.ppermute(block, axis, route)  7.34 us
    unnamed x17, local copies, waits for them, and re-layouts  5.97 us
    dot_general x1, matrix products, apply_mix(): jnp.einsum('ablk,laibj->kaibj', mix_blocks, spread_state, precision=highest)  4.5 us
    all_to_all x1, starting transfers between devices, shards(): lax.all_to_all(spread, 'mem', split_axis=1, concat_axis=0, tiled=True)  4.35 us
  transfers between devices with their start and end apart: 5, of which 0 were waited for; matrix products, arithmetic and copies ran while one was open for 32% of the time, Pallas kernels for 0%

commit v1 on v0

--- a/solution.py
+++ b/solution.py
@@ -138,7 +138,10 @@
         totals = lax.fori_loop(opening, opening + (filled + stride - 1) // stride, visit, totals)
     mixing = transform(totals[0], totals[1], members)
     analysis = apply_mix(gathered_state[:, 0, :], mixing, rows_dev)
-    returned = lax.all_to_all(analysis[:, None, :], "mem", split_axis=0, concat_axis=1, tiled=True)
+    own = analysis[:, None, :]
+    parts = jnp.split(own, lax.axis_size("mem"), axis=0)
+    got = lax.all_to_all(jnp.stack(parts), "mem", 0, 0)
+    returned = jnp.concatenate(got, axis=1)
     return returned.reshape(mem_dev, 1, cell_count)
 
 

time: 105 us -> 140 us (1.33)
  local copies, waits for them, and re-layouts: 27.2 us -> 62.3 us
    split x0 -> x5, local copies, waits for them, and re-layouts: none -> 30.8 us  [shards(): parts = jnp.split(own, lax.axis_size('mem'), axis=0)]
    another operation x2 -> x6, local copies, waits for them, and re-layouts: 3.16 us -> 8.83 us  [the longest x5 7.66 us: shards(): got = lax.all_to_all(jnp.stack(parts), 'mem', 0, 0)]
    unnamed x17 -> x15, local copies, waits for them, and re-layouts: 5.97 us -> 5.2 us
  transfers between devices with their start and end apart: 5 -> 5, of which waited for: 0 -> 0; matrix products, arithmetic and copies ran while one was open for 32% -> 23% of each run, Pallas kernels for 0% -> 0%
where the time goes in v1:
time: 140 us; the launch traced here: 139 us
  local copies, waits for them, and re-layouts  62.3 us (44%)
  matrix products  28.2 us (20%)
  blocking collectives  24.2 us (17%)
  starting transfers between devices  11.7 us (8%)
  other arithmetic  6.94 us (5%)
  between operations  5.14 us (4%)
    split x5, local copies, waits for them, and re-layouts, shards(): parts = jnp.split(own, lax.axis_size('mem'), axis=0)  30.8 us
    all_to_all x1, blocking collectives, shards(): got = lax.all_to_all(jnp.stack(parts), 'mem', 0, 0)  13.5 us
    all_gather x1, blocking collectives, shards(): ensemble = lax.all_gather(own_obs, 'mem', axis=0, tiled=True)  10.8 us
    dot_general x6, matrix products, add_block(): jnp.einsum('pkj,lj->pkl', weighted, spread_obs, precision=highest)  8.79 us
    another operation x2, local copies, waits for them, and re-layouts, apply_mix(): band_state.reshape(members, row_blocks, BLOCK, col_blocks, BLOCK)  8.62 us
    another operation x5, local copies, waits for them, and re-layouts, shards(): got = lax.all_to_all(jnp.stack(parts), 'mem', 0, 0)  7.66 us
    ppermute x4, starting transfers between devices, shifted(): return lax.ppermute(block, axis, route)  7.34 us
    unnamed x15, local copies, waits for them, and re-layouts  5.2 us
  transfers between devices with their start and end apart: 5, of which 0 were waited for; matrix products, arithmetic and copies ran while one was open for 23% of the time, Pallas kernels for 0%

profile of v1, /device:TPU:5, one launch (start us, length us, event | category | flops | bytes accessed | tf_op | source)
XLA Modules:
  0.0 139.2 jit_solution(3676575363834728565)
XLA Ops:
  2.1 5.1 %copy.36 = f32[5,1,12960]{0,2,1:T(8,128)} copy(f32[5,1,12960]{2,1,0:T(1,128)} %param.16) | data formatting | bytes 518400 | tf_op args[0]
  7.2 3.6 %gather_fusion = f32[256,5]{1,0:T(8,128)S(1)} fusion(f32[5,12960]{0,1:T(8,128)} %bitcast.208, s32[1024]{0:T(1024)S(1)} %pad_clamp_fusion), kind=kCustom, calls=%fused_computation | custom fusion | bytes 11264 | tf_op jit(solution)/shard_map/jit(_take)/gather | solution.py:100
  10.9 10.8 %all-gather = f32[4,5,256]{2,1,0:T(8,128)S(1)} all-gather(f32[1,5,256]{2,1,0:T(8,128)S(1)} %copy.37), channel_id=1, replica_groups=mesh['mem'=4,'tile'=8] {'mem'}, dimensions={0}, use_global_device_ids=true | all-gather | bytes 25600 | tf_op jit(solution)/shard_map/all_gather | solution.py:107
  24.0 3.8 %collective-permute-start.1 = (f32[24,256]{1,0:T(8,128)S(1)}, f32[24,256]{1,0:T(8,128)S(1)}, u32[]{:S(2)}, u32[]{:S(2)}) collective-permute-start(f32[24,256]{1,0:T(8,128)S(1)} %concatenate.6), channel_id=1, source_target_pairs={{1,0},{2,1},{3,2},{4,3},{5,4},{6,5},{7,6},{0,7},{9,8},{10,9},{11,1... | collective-permute-start | bytes 73736 | tf_op jit(solution)/shard_map/ppermute | solution.py:16
  27.8 2.0 %collective-permute-start = (f32[24,256]{1,0:T(8,128)S(1)}, f32[24,256]{1,0:T(8,128)S(1)}, u32[]{:S(2)}, u32[]{:S(2)}) collective-permute-start(f32[24,256]{1,0:T(8,128)S(1)} %concatenate.6), channel_id=1, source_target_pairs={{7,0},{0,1},{1,2},{2,3},{3,4},{4,5},{5,6},{6,7},{15,8},{8,9},{9,10... | collective-permute-start | bytes 73736 | tf_op jit(solution)/shard_map/ppermute | solution.py:16
  31.5 4.3 %all-to-all-start = ((f32[5,4,3240]{2,0,1:T(8,128)}), f32[5,4,3240]{2,0,1:T(8,128)S(1)}, u32[]{:S(2)}, u32[]{:S(2)}) async-start(f32[5,4,3240]{2,0,1:T(8,128)} %copy.33), calls=%async_computation | async-start | bytes 851968 | tf_op jit(solution)/shard_map/all_to_all | solution.py:116
  42.9 2.6 %while.65 = (s32[]{:T(128)}, f32[40,20,20]{0,2,1:T(8,128)S(1)}, f32[40,20]{0,1:T(8,128)S(1)}, s32[]{:T(128)}, f32[4,1280]{1,0:T(4,128)S(1)}, /*index=5*/f32[]{:T...) while((s32[]{:T(128)}, f32[40,20,20]{0,2,1:T(8,128)S(1)}, ...), condition=%wide.region_4.5_spmd.clone, body=%wide.region_2.4_spmd.clone.sunk | while | flops 26103460 | bytes 275183 | solution.py:138
  45.5 2.6 %while.66 = (s32[]{:T(128)}, f32[40,20,20]{0,2,1:T(8,128)S(1)}, f32[40,20]{0,1:T(8,128)S(1)}, s32[]{:T(128)}, f32[4,1280]{1,0:T(4,128)S(1)}, /*index=5*/f32[]{:T...) while((s32[]{:T(128)}, f32[40,20,20]{0,2,1:T(8,128)S(1)}, ...), condition=%wide.region_8.9_spmd.clone, body=%wide.region_6.8_spmd.clone.sunk | while | flops 26103460 | bytes 275183 | solution.py:138
  48.1 2.6 %while.67 = (s32[]{:T(128)}, f32[40,20,20]{0,2,1:T(8,128)S(1)}, f32[40,20]{0,1:T(8,128)S(1)}, s32[]{:T(128)}, f32[4,1280]{1,0:T(4,128)S(1)}, /*index=5*/f32[]{:T...) while((s32[]{:T(128)}, f32[40,20,20]{0,2,1:T(8,128)S(1)}, ...), condition=%wide.region_12.13_spmd.clone, body=%wide.region_10.12_spmd.clone.sunk | while | flops 26103460 | bytes 275183 | solution.py:138
  50.7 5.2 %while.68 = (s32[]{:T(128)}, f32[40,20,20]{0,2,1:T(8,128)S(1)}, f32[40,20]{0,1:T(8,128)S(1)}, s32[]{:T(128)}, f32[4,1280]{1,0:T(4,128)S(1)}, /*index=5*/f32[]{:T...) while((s32[]{:T(128)}, f32[40,20,20]{0,2,1:T(8,128)S(1)}, ...), condition=%wide.region_16.17_spmd.clone, body=%wide.region_14.16_spmd.clone.sunk | while | flops 26103460 | bytes 275183 | solution.py:138
  55.9 2.8 %while.69 = (s32[]{:T(128)}, f32[40,20,20]{0,2,1:T(8,128)S(1)}, f32[40,20]{0,1:T(8,128)S(1)}, s32[]{:T(128)}, f32[4,1280]{1,0:T(4,128)S(1)}, /*index=5*/f32[]{:T...) while((s32[]{:T(128)}, f32[40,20,20]{0,2,1:T(8,128)S(1)}, ...), condition=%wide.region_20.21_spmd.clone, body=%wide.region_18.20_spmd.clone.sunk | while | flops 26103460 | bytes 275183 | solution.py:138
  72.8 3.7 %reshape_squeeze.3 = f32[20,8,9,5,9]{4,3,2,1,0:T(8,128)} reshape(f32[4,5,1,3240]{3,1,0,2:T(8,128)S(1)} %bitcast.209) | data formatting | bytes 518400 | tf_op jit(solution)/shard_map/reshape;squeeze | solution.py:76
  76.5 4.9 %copy.35 = f32[20,8,9,5,9]{0,4,2,3,1:T(8,128)S(1)} copy(f32[20,8,9,5,9]{4,3,2,1,0:T(8,128)} %reshape_squeeze.3) | data formatting | bytes 518400 | tf_op jit(solution)/shard_map/reshape;squeeze | solution.py:76
  81.4 4.6 %bitcast_add_fusion.5 = f32[20,8,9,5,9]{0,4,2,3,1:T(8,128)S(1)} fusion(f32[8,5,20,20,1]{3,2,4,1,0:T(8,128)S(1)} %bitcast.211, f32[20,8,9,5,9]{0,4,2,3,1:T(8,128)S(1)} %copy.35, f32[8,9,5,9]{3,1,2,0:T(8,128)} %copy.34), kind=kOutput, calls=%fused_computation.141 | convolution fusion | flops 15681600 | bytes 595360 | tf_op jit(solution)/shard_map/ablk,laibj->kaibj/dot_general | solution.py:81
  86.0 5.7 %fusion.118 = (f32[5,8,9,5,9]{0,4,2,3,1:T(8,128)}, f32[5,8,9,5,9]{0,4,2,3,1:T(8,128)}, f32[5,8,9,5,9]{0,4,2,3,1:T(8,128)}, f32[5,8,9,5,9]{0,4,2,3,1:T(8,128)S(1)}) fusion(f32[20,8,9,5,9]{0,4,2,3,1:T(8,128)S(1)} %bitcast_add_fusion.5), kind=kLoop, calls=%fused_computation.196 | loop fusion | bytes 518400 | tf_op jit(solution)/shard_map/split | solution.py:142
  91.7 6.6 %copy.40 = f32[5,8,9,5,9]{4,3,2,1,0:T(8,128)} copy(f32[5,8,9,5,9]{0,4,2,3,1:T(8,128)} %get-tuple-element.487) | data formatting | bytes 129600 | tf_op jit(solution)/shard_map/split | solution.py:142
  98.3 1.8 %stack.18 = f32[1,5,1,3240]{3,1,2,0:T(8,128)S(1)} reshape(f32[5,8,9,5,9]{4,3,2,1,0:T(8,128)} %copy.40) | data formatting | bytes 129600 | tf_op jit(solution)/shard_map/stack | solution.py:143
  100.2 6.5 %copy.43 = f32[5,8,9,5,9]{4,3,2,1,0:T(8,128)} copy(f32[5,8,9,5,9]{0,4,2,3,1:T(8,128)} %get-tuple-element.488) | data formatting | bytes 129600 | tf_op jit(solution)/shard_map/split | solution.py:142
  106.7 1.8 %stack.21 = f32[1,5,1,3240]{3,1,2,0:T(8,128)S(1)} reshape(f32[5,8,9,5,9]{4,3,2,1,0:T(8,128)} %copy.43) | data formatting | bytes 129600 | tf_op jit(solution)/shard_map/stack | solution.py:143
  108.5 6.5 %copy.42 = f32[5,8,9,5,9]{4,3,2,1,0:T(8,128)} copy(f32[5,8,9,5,9]{0,4,2,3,1:T(8,128)} %get-tuple-element.489) | data formatting | bytes 129600 | tf_op jit(solution)/shard_map/split | solution.py:142
  115.1 1.8 %stack.20 = f32[1,5,1,3240]{3,1,2,0:T(8,128)S(1)} reshape(f32[5,8,9,5,9]{4,3,2,1,0:T(8,128)} %copy.42) | data formatting | bytes 129600 | tf_op jit(solution)/shard_map/stack | solution.py:143
  116.9 5.4 %copy.41 = f32[5,8,9,5,9]{4,3,2,1,0:T(8,128)} copy(f32[5,8,9,5,9]{0,4,2,3,1:T(8,128)S(1)} %get-tuple-element.490) | data formatting | bytes 129600 | tf_op jit(solution)/shard_map/split | solution.py:142
  122.3 1.8 %stack.19 = f32[1,5,1,3240]{3,1,2,0:T(8,128)S(1)} reshape(f32[5,8,9,5,9]{4,3,2,1,0:T(8,128)} %copy.41) | data formatting | bytes 129600 | tf_op jit(solution)/shard_map/stack | solution.py:143
  124.5 13.5 %all_to_all.20 = f32[4,5,1,3240]{3,2,1,0:T(1,128)S(1)} all-to-all(f32[4,5,1,3240]{3,2,1,0:T(1,128)S(1)} %copy.44), channel_id=1, replica_groups=mesh['mem'=4,'tile'=8] {'mem'}, dimensions={0} | all-to-all | bytes 518400 | tf_op jit(solution)/shard_map/all_to_all | solution.py:143
  (154 shorter events, 38.9 us)
Async XLA Ops:
  2.0 19.7 %copy-start.1 = (s32[1,256]{1,0:T(1,128)S(1)}, s32[1,256]{1,0:T(1,128)}, u32[]{:S(2)}) copy-start(s32[1,256]{1,0:T(1,128)} %param.17) | copy-start | bytes 3076
  2.0 19.7 %copy-start.2 = (f32[1,256]{1,0:T(1,128)S(1)}, f32[1,256]{1,0:T(1,128)}, u32[]{:S(2)}) copy-start(f32[1,256]{1,0:T(1,128)} %param.20) | copy-start | bytes 3076
  2.1 20.4 %copy-start.3 = (f32[1,256]{1,0:T(1,128)S(1)}, f32[1,256]{1,0:T(1,128)}, u32[]{:S(2)}) copy-start(f32[1,256]{1,0:T(1,128)} %param.19) | copy-start | bytes 3076
  2.1 27.8 %copy-start = (f32[5,1,12960]{2,1,0:T(1,128)S(1)}, f32[5,1,12960]{2,1,0:T(1,128)}, u32[]{:S(2)}) copy-start(f32[5,1,12960]{2,1,0:T(1,128)} %param.16) | copy-start | bytes 777604
  22.5 14.8 %collective-permute-start.3 = (f32[24,256]{1,0:T(8,128)S(1)}, f32[24,256]{1,0:T(8,128)S(1)}, u32[]{:S(2)}, u32[]{:S(2)}) collective-permute-start(f32[24,256]{1,0:T(8,128)S(1)} %concatenate.6), channel_id=1, source_target_pairs={{2,0},{3,1},{4,2},{5,3},{6,4},{7,5},{0,6},{1,7},{10,8},{11,9},{12,... | collective-permute-start | bytes 73736 | tf_op jit(solution)/shard_map/ppermute | solution.py:16
  23.7 14.3 %collective-permute-start.2 = (f32[24,256]{1,0:T(8,128)S(1)}, f32[24,256]{1,0:T(8,128)S(1)}, u32[]{:S(2)}, u32[]{:S(2)}) collective-permute-start(f32[24,256]{1,0:T(8,128)S(1)} %concatenate.6), channel_id=1, source_target_pairs={{6,0},{7,1},{0,2},{1,3},{2,4},{3,5},{4,6},{5,7},{14,8},{15,9},{8,1... | collective-permute-start | bytes 73736 | tf_op jit(solution)/shard_map/ppermute | solution.py:16
  24.0 14.6 %collective-permute-start.1 = (f32[24,256]{1,0:T(8,128)S(1)}, f32[24,256]{1,0:T(8,128)S(1)}, u32[]{:S(2)}, u32[]{:S(2)}) collective-permute-start(f32[24,256]{1,0:T(8,128)S(1)} %concatenate.6), channel_id=1, source_target_pairs={{1,0},{2,1},{3,2},{4,3},{5,4},{6,5},{7,6},{0,7},{9,8},{10,9},{11,1... | collective-permute-start | bytes 73736 | tf_op jit(solution)/shard_map/ppermute | solution.py:16
  27.8 13.4 %collective-permute-start = (f32[24,256]{1,0:T(8,128)S(1)}, f32[24,256]{1,0:T(8,128)S(1)}, u32[]{:S(2)}, u32[]{:S(2)}) collective-permute-start(f32[24,256]{1,0:T(8,128)S(1)} %concatenate.6), channel_id=1, source_target_pairs={{7,0},{0,1},{1,2},{2,3},{3,4},{4,5},{5,6},{6,7},{15,8},{8,9},{9,10... | collective-permute-start | bytes 73736 | tf_op jit(solution)/shard_map/ppermute | solution.py:16
  31.5 40.2 %all-to-all-start = ((f32[5,4,3240]{2,0,1:T(8,128)}), f32[5,4,3240]{2,0,1:T(8,128)S(1)}, u32[]{:S(2)}, u32[]{:S(2)}) async-start(f32[5,4,3240]{2,0,1:T(8,128)} %copy.33), calls=%async_computation | async-start | bytes 851968 | tf_op jit(solution)/shard_map/all_to_all | solution.py:116
